TPU v7x, 32 devices: a whole 2x2x4 slice. The times are simulated.
32 devices in a mesh: dp: 8 (over y, x, core), tensor: 4 (over z).
Axes of the slice: x: 2, y: 2, z: 4, core: 2. Of those that a mesh axis runs over, the one named last changes fastest.
Arguments:
- tokens: bfloat16 [16384, 1536], P('dp'), may hold values from -6 to 6
- cotangent: bfloat16 [16384, 1536], P('dp'), may hold values from -6 to 6
- destination: int32 [16384], P('dp'), may hold values from 0 to 16383, as said below
- lengths: int32 [8, 4], P('dp'), may hold values from 1 to 1024, 2048 in all within a row
- norm_gain: float32 [1536], replicated, may hold values from 0.1 to 1.9
- inner_weight: float32 [1536, 2, 3072], P('dp', None, 'tensor'), may hold values from -0.15625 to 0.15625
- shared_weight: float32 [1536, 256], P('dp'), may hold values from -0.15625 to 0.15625
- step_weight: float32 [1536, 48], P('dp', 'tensor'), may hold values from -0.15625 to 0.15625
- filter_weight: float32 [4, 3072], P(None, 'tensor'), may hold values from -3 to 3
- filter_bias: float32 [3072], P('tensor'), may hold values from -3 to 3
- shared_filter: float32 [4, 256], replicated, may hold values from -3 to 3
- shared_filter_bias: float32 [256], replicated, may hold values from -3 to 3
- step_bias: float32 [48], P('tensor'), may hold values from -6 to -2
- decay_log: float32 [48], P('tensor'), may hold values from 0 to 2.77
- skip_gain: float32 [48], P('tensor'), may hold values from 0.5 to 1.5
- gate_gain: float32 [3072], P('tensor'), may hold values from 0.1 to 1.9
- out_weight: float32 [1536, 3072], P('dp', 'tensor'), may hold values from -0.109375 to 0.109375
Outputs:
- layer_out: bfloat16 [16384, 1536], P('dp')
- input_grad: bfloat16 [16384, 1536], P('dp')
- norm_gain_grad: float32 [1536], replicated
- inner_weight_grad: float32 [1536, 2, 3072], P('dp', None, 'tensor')
- shared_weight_grad: float32 [1536, 256], P('dp')
- step_weight_grad: float32 [1536, 48], P('dp', 'tensor')
- filter_weight_grad: float32 [4, 3072], P(None, 'tensor')
- filter_bias_grad: float32 [3072], P('tensor')
- shared_filter_grad: float32 [4, 256], replicated
- shared_filter_bias_grad: float32 [256], replicated
- step_bias_grad: float32 [48], P('tensor')
- decay_log_grad: float32 [48], P('tensor')
- skip_gain_grad: float32 [48], P('tensor')
- gate_gain_grad: float32 [3072], P('tensor')
- out_weight_grad: float32 [1536, 3072], P('dp', 'tensor')
Inputs may be any that keep to these rules, and one draw needn't show every extreme that they name: destination is a permutation. The tokens at given positions s * 2048 to (s + 1) * 2048 - 1 that go to work block w take exactly the work positions w * 2048 + s * 256 to w * 2048 + (s + 1) * 256 - 1. `lengths`: each row sums to 2048, and its longest sequence has exactly 1024 tokens.
All inputs are finite; a program needn't handle non-finite values.
Results may differ from a plain program's by a relative error of at most 0.012.
Values may be sent and summed in bfloat16 or wider, within the bound.
No kernel may reach another device: no remote copies, remote signals or barrier semaphores. Data moves between devices by JAX's collectives and lax.ppermute only.
A program may use at most 256 MiB of HBM per device.

v0:
```python
import jax
import jax.numpy as jnp
from jax import lax
from jax.sharding import PartitionSpec as P

INNER = 3072
SPAN = 256
EPSILON = 1e-05
PRECISE = lax.Precision.HIGHEST


def segments_of(lengths, row_count):
    seq_ends = jnp.cumsum(lengths)
    seq_starts = seq_ends - lengths
    places = jnp.arange(row_count, dtype=jnp.int32)
    segment = jnp.sum((places[:, None] >= seq_ends[None, :]).astype(jnp.int32), axis=1)
    belongs = segment[:, None] == jnp.arange(lengths.shape[0], dtype=jnp.int32)[None, :]
    position = places - jnp.sum(jnp.where(belongs, seq_starts[None, :], 0), axis=1)
    return (segment, position)


def causal_filter(signal, kernel, offset_bias, position):
    result = offset_bias + kernel[0] * signal
    for offset in range(1, kernel.shape[0]):
        shifted = jnp.pad(signal, ((offset, 0), (0, 0)))[: signal.shape[0]]
        allowed = (position >= offset).astype(signal.dtype)
        result = result + kernel[offset] * shifted * allowed[:, None]
    return result


def mixer(
    inputs,
    shared,
    step_raw,
    filter_weight,
    filter_bias,
    shared_filter,
    shared_filter_bias,
    step_bias,
    decay_log,
    skip_gain,
    segment,
    position,
):
    row_count = inputs.shape[0]
    heads_here = step_bias.shape[0]
    state_size = shared.shape[1] // 2
    values = jax.nn.silu(causal_filter(inputs, filter_weight, filter_bias, position)).reshape(
        row_count, heads_here, -1
    )
    factors = jax.nn.silu(causal_filter(shared, shared_filter, shared_filter_bias, position))
    writes = factors[:, :state_size]
    read_vectors = factors[:, state_size:]
    step_size = jax.nn.softplus(step_raw + step_bias)
    log_decay = -step_size * jnp.exp(decay_log)
    blocks = row_count // SPAN
    causal = jnp.arange(SPAN)[:, None] >= jnp.arange(SPAN)[None, :]

    def blocked(whole_array):
        return whole_array.reshape((blocks, SPAN) + whole_array.shape[1:])

    def span_step(state_carry, block_item):
        memory, last_segment = state_carry
        value_blk, write_blk, read_blk, size_blk, decay_blk, segment_blk = block_item
        cumulative = jnp.cumsum(decay_blk, axis=0).T
        inside = causal & (segment_blk[:, None] == segment_blk[None, :])
        spread = cumulative[:, :, None] - cumulative[:, None, :]
        decays = jnp.exp(jnp.where(inside[None], spread, -jnp.inf))
        scores = jnp.dot(read_blk, write_blk.T, precision=PRECISE)
        mixing = scores[None] * decays * size_blk.T[:, None, :]
        local_out = jnp.einsum("hts,shp->thp", mixing, value_blk, precision=PRECISE)
        carried = (segment_blk == last_segment).astype(value_blk.dtype)
        entering = jnp.exp(cumulative).T * carried[:, None]
        remote_out = (
            jnp.einsum("tn,hnp->thp", read_blk, memory, precision=PRECISE) * entering[:, :, None]
        )
        block_out = local_out + remote_out + skip_gain[None, :, None] * value_blk
        end_segment = segment_blk[-1]
        closing = (segment_blk == end_segment).astype(value_blk.dtype)
        weights = jnp.exp(cumulative[:, -1:] - cumulative) * size_blk.T * closing[None, :]
        added_state = jnp.einsum("sn,hs,shp->hnp", write_blk, weights, value_blk, precision=PRECISE)
        keeping = jnp.exp(cumulative[:, -1]) * (last_segment == end_segment).astype(value_blk.dtype)
        memory = memory * keeping[:, None, None] + added_state
        return ((memory, end_segment), block_out)

    initial = (jnp.zeros((heads_here, state_size, values.shape[2]), values.dtype), jnp.int32(-1))
    unused, outputs = lax.scan(
        jax.checkpoint(span_step),
        initial,
        (
            blocked(values),
            blocked(writes),
            blocked(read_vectors),
            blocked(step_size),
            blocked(log_decay),
            blocked(segment),
        ),
    )
    return outputs.reshape(row_count, -1)


def prenorm(hidden_in, norm_gain):
    scale = lax.rsqrt(jnp.mean(hidden_in * hidden_in, axis=1, keepdims=True) + EPSILON)
    return hidden_in * scale * norm_gain


def on_device(
    tokens,
    cotangent,
    destination,
    lengths,
    norm_gain,
    inner_weight,
    shared_weight,
    step_weight,
    filter_weight,
    filter_bias,
    shared_filter,
    shared_filter_bias,
    step_bias,
    decay_log,
    skip_gain,
    gate_gain,
    out_weight,
):
    row_count = tokens.shape[0]
    model_width = tokens.shape[1]
    group_rows = row_count // lax.axis_size("dp")
    my_index = lax.axis_index("dp")
    target_block = destination // row_count
    send_slot = (
        target_block * group_rows + (destination - target_block * row_count) - my_index * group_rows
    )
    send_order = (
        jnp.zeros((row_count,), jnp.int32).at[send_slot].set(jnp.arange(row_count, dtype=jnp.int32))
    )
    send_tokens = tokens[send_order]
    send_cot = cotangent[send_order]
    work_tokens, work_cot = (
        lax.all_to_all(send_tokens, "dp", split_axis=0, concat_axis=0, tiled=True),
        lax.all_to_all(send_cot, "dp", split_axis=0, concat_axis=0, tiled=True),
    )
    inner_full, shared_full, step_full, out_full = (
        lax.all_gather(inner_weight.astype(jnp.bfloat16), "dp", axis=0, tiled=True),
        lax.all_gather(shared_weight.astype(jnp.bfloat16), "dp", axis=0, tiled=True),
        lax.all_gather(step_weight.astype(jnp.bfloat16), "dp", axis=0, tiled=True),
        lax.all_gather(out_weight.astype(jnp.bfloat16), "dp", axis=0, tiled=True),
    )
    col_share = model_width // lax.axis_size("tensor")
    column = lax.axis_index("tensor") * col_share
    hidden_in = work_tokens.astype(jnp.float32)
    segment, position = segments_of(lengths[0], row_count)
    normed, pull_norm = jax.vjp(prenorm, hidden_in, norm_gain)
    normed_low = normed.astype(jnp.bfloat16)
    inner_flat = inner_full.reshape(inner_full.shape[0], -1)
    both = jnp.dot(normed_low, inner_flat, preferred_element_type=jnp.float32)
    half_width = both.shape[1] // 2
    gate_in = both[:, :half_width]
    inputs = both[:, half_width:]
    shared = jnp.dot(normed_low, shared_full, preferred_element_type=jnp.float32)
    step_raw = jnp.dot(normed_low, step_full, preferred_element_type=jnp.float32)

    def local_mixer(
        inputs,
        shared,
        step_raw,
        filter_weight,
        filter_bias,
        shared_filter,
        shared_filter_bias,
        step_bias,
        decay_log,
        skip_gain,
    ):
        return mixer(
            inputs,
            shared,
            step_raw,
            filter_weight,
            filter_bias,
            shared_filter,
            shared_filter_bias,
            step_bias,
            decay_log,
            skip_gain,
            segment,
            position,
        )

    mixed_in, pull_mixer = jax.vjp(
        local_mixer,
        inputs,
        shared,
        step_raw,
        filter_weight,
        filter_bias,
        shared_filter,
        shared_filter_bias,
        step_bias,
        decay_log,
        skip_gain,
    )
    gate_sig = jax.nn.sigmoid(gate_in)
    gate_act = gate_in * gate_sig
    gated = mixed_in * gate_act
    square_sum = lax.psum(jnp.sum(gated * gated, axis=1), "tensor")
    gate_scale = lax.rsqrt(square_sum / INNER + EPSILON)[:, None]
    gate_normed = (gated * gate_scale * gate_gain).astype(jnp.bfloat16)
    partial_out = jnp.einsum("ti,di->td", gate_normed, out_full, preferred_element_type=jnp.float32)
    branch = lax.psum(partial_out, "tensor")
    layer_work = (hidden_in + branch).astype(jnp.bfloat16)
    part_out = lax.dynamic_slice_in_dim(layer_work, column, col_share, 1)
    out_grad = jnp.einsum("td,ti->di", work_cot, gate_normed, preferred_element_type=jnp.float32)
    normed_grad = jnp.einsum("td,di->ti", work_cot, out_full, preferred_element_type=jnp.float32)
    gate_gain_grad = jnp.sum(normed_grad * gated * gate_scale, axis=0)
    scaled_grad = normed_grad * gate_gain
    cross_sum = lax.psum(jnp.sum(scaled_grad * gated, axis=1), "tensor")
    gated_grad = gate_scale * scaled_grad - gated * gate_scale**3 * (cross_sum / INNER)[:, None]
    mixed_grad = gated_grad * gate_act
    gate_in_grad = gated_grad * mixed_in * gate_sig * (1.0 + gate_in * (1.0 - gate_sig))
    (
        inputs_grad,
        shared_part,
        step_raw_grad,
        filter_weight_grad,
        filter_bias_grad,
        shared_filter_part,
        shared_bias_part,
        step_bias_grad,
        decay_log_grad,
        skip_gain_grad,
    ) = pull_mixer(mixed_grad)
    shared_grad, shared_filter_grad, shared_filter_bias_grad = lax.psum(
        (shared_part, shared_filter_part, shared_bias_part), "tensor"
    )
    both_low = jnp.concatenate([gate_in_grad, inputs_grad], axis=1).astype(jnp.bfloat16)
    shared_low = shared_grad.astype(jnp.bfloat16)
    step_low = step_raw_grad.astype(jnp.bfloat16)
    input_part = jnp.einsum("tk,dk->td", both_low, inner_flat, preferred_element_type=jnp.float32)
    input_part = input_part + jnp.einsum(
        "tk,dk->td", step_low, step_full, preferred_element_type=jnp.float32
    )
    normed_back = lax.psum(input_part, "tensor")
    normed_back = normed_back + jnp.einsum(
        "tk,dk->td", shared_low, shared_full, preferred_element_type=jnp.float32
    )
    input_norm_grad, norm_gain_grad = pull_norm(normed_back)
    input_work = (input_norm_grad + work_cot.astype(jnp.float32)).astype(jnp.bfloat16)
    part_grad = lax.dynamic_slice_in_dim(input_work, column, col_share, 1)
    inner_grad = jnp.einsum(
        "td,tk->dk", normed_low, both_low, preferred_element_type=jnp.float32
    ).reshape(inner_full.shape)
    shared_weight_grad = jnp.einsum(
        "td,tk->dk", normed_low, shared_low, preferred_element_type=jnp.float32
    )
    step_weight_grad = jnp.einsum(
        "td,tk->dk", normed_low, step_low, preferred_element_type=jnp.float32
    )
    inner_grad, shared_weight_grad, step_weight_grad, out_grad = (
        lax.psum_scatter(inner_grad, "dp", scatter_dimension=0, tiled=True),
        lax.psum_scatter(shared_weight_grad, "dp", scatter_dimension=0, tiled=True),
        lax.psum_scatter(step_weight_grad, "dp", scatter_dimension=0, tiled=True),
        lax.psum_scatter(out_grad, "dp", scatter_dimension=0, tiled=True),
    )
    (
        norm_gain_grad,
        filter_weight_grad,
        filter_bias_grad,
        shared_filter_grad,
        shared_filter_bias_grad,
        step_bias_grad,
        decay_log_grad,
        skip_gain_grad,
        gate_gain_grad,
    ) = lax.psum(
        (
            norm_gain_grad,
            filter_weight_grad,
            filter_bias_grad,
            shared_filter_grad,
            shared_filter_bias_grad,
            step_bias_grad,
            decay_log_grad,
            skip_gain_grad,
            gate_gain_grad,
        ),
        "dp",
    )
    part_out, part_grad = (
        lax.all_to_all(part_out, "dp", split_axis=0, concat_axis=0, tiled=True),
        lax.all_to_all(part_grad, "dp", split_axis=0, concat_axis=0, tiled=True),
    )
    back_out, back_grad = (
        lax.all_gather(part_out, "tensor", axis=1, tiled=True),
        lax.all_gather(part_grad, "tensor", axis=1, tiled=True),
    )
    layer_out = back_out[send_slot]
    input_grad = back_grad[send_slot]
    return (
        layer_out,
        input_grad,
        norm_gain_grad,
        inner_grad,
        shared_weight_grad,
        step_weight_grad,
        filter_weight_grad,
        filter_bias_grad,
        shared_filter_grad,
        shared_filter_bias_grad,
        step_bias_grad,
        decay_log_grad,
        skip_gain_grad,
        gate_gain_grad,
        out_grad,
    )


def solution(mesh):
    in_specs = (
        P("dp", None),
        P("dp", None),
        P("dp"),
        P("dp", None),
        P(),
        P("dp", None, "tensor"),
        P("dp", None),
        P("dp", "tensor"),
        P(None, "tensor"),
        P("tensor"),
        P(),
        P(),
        P("tensor"),
        P("tensor"),
        P("tensor"),
        P("tensor"),
        P("dp", "tensor"),
    )
    out_specs = (
        P("dp", None),
        P("dp", None),
        P(),
        P("dp", None, "tensor"),
        P("dp", None),
        P("dp", "tensor"),
        P(None, "tensor"),
        P("tensor"),
        P(),
        P(),
        P("tensor"),
        P("tensor"),
        P("tensor"),
        P("tensor"),
        P("dp", "tensor"),
    )
    return jax.shard_map(
        on_device, mesh=mesh, in_specs=in_specs, out_specs=out_specs, check_vma=False
    )
```

profile of v0, /device:TPU:0, one launch (start us, length us, event | category | flops | bytes accessed | tf_op | source)
XLA Modules:
  0.0 2527.5 jit_solution(8638867920375196014)
XLA Ops:
  19.1 17.3 gather_fusion
  42.7 88.8 %all-gather = bf16[8,192,12]{1,2,0:T(8,128)(2,1)S(1)} all-gather(bf16[1,192,12]{1,2,0:T(8,128)(2,1)S(1)} %convert_bitcast_fusion), channel_id=1, replica_groups=mesh['dp'=8,'tensor'=4] {'dp'}, dimensions={0}, use_global_device_ids=true | all-gather | bytes 41472 | tf_op jit(solution)/shard_map/all_gather | solution.py:146
  131.8 16.9 gather_fusion.2
  240.2 294.4 %while.47 = (s32[]{:T(128)}, f32[12,128,64]{1,2,0:T(8,128)S(1)}, s32[]{:T(128)}, f32[8,256,12,64]{1,0,3,2:T(8,128)}, f32[8,12,128,64]{2,3,1,0:T(8,128)}, /*index...) while((s32[]{:T(128)}, f32[12,128,64]{1,2,0:T(8,128)S(1)}, ...), condition=%wide.region_8.9_spmd.clone, body=%wide.region_5.8_spmd.clone.sunk | while | flops 1313649664 | bytes 11765497 | solution.py:87
  254.0 18.5 dynamic_update_slice.85
  290.8 18.5 dynamic_update_slice.85
  327.6 18.5 dynamic_update_slice.85
  364.4 18.5 dynamic_update_slice.85
  401.2 18.5 dynamic_update_slice.85
  438.0 18.5 dynamic_update_slice.85
  474.8 18.5 dynamic_update_slice.85
  511.6 18.5 dynamic_update_slice.85
  624.5 466.0 %while.48 = (s32[]{:T(128)}, f32[12]{0:T(128)}, f32[12,128,64]{1,2,0:T(8,128)S(1)}, f32[8,256,12,64]{1,0,3,2:T(8,128)}, f32[8,256,128]{2,1,0:T(8,128)}, /*index=...) while((s32[]{:T(128)}, f32[12]{0:T(128)}, ...), condition=%wide.region_27.28_spmd.clone, body=%wide.region_14.27_spmd.clone.sunk | while | flops 3037355008 | bytes 28656244 | solution.py:87
  657.0 18.5 dynamic_update_slice.89
  715.2 18.5 dynamic_update_slice.89
  773.4 18.5 dynamic_update_slice.89
  831.5 18.5 dynamic_update_slice.89
  889.7 18.5 dynamic_update_slice.89
  947.8 18.5 dynamic_update_slice.89
  1006.0 18.5 dynamic_update_slice.89
  1064.2 18.5 dynamic_update_slice.89
  1219.2 147.4 %all-reduce.31 = (bf16[2048,256]{1,0:T(8,128)(2,1)}, f32[4,256]{1,0:T(4,128)S(1)}, f32[256]{0:T(256)S(1)}) all-reduce(f32[2048,256]{1,0:T(8,128)S(1)} %fusion.111, f32[4,256]{1,0:T(4,128)S(1)} %pad_add_fusion.1, f32[256]{0:T(256)S(1)} %get-tuple-element.895), channel_id=1, replica_groups=mesh['dp'=8,'tensor'=4] {'tensor'}, use_global_device_ids=true, to_apply=%region_29.30 | all-reduce | flops 525568 | bytes 3155968 | tf_op jit(solution)/shard_map/psum | solution.py:233
  1366.6 702.3 %all-reduce.30.cloned.1.call-done = (f32[2048,1536]{1,0:T(8,128)}, f32[2048,1536]{1,0:T(8,128)}) async-done(((f32[2048,1536]{1,0:T(8,128)}, f32[2048,1536]{1,0:T(8,128)}), (f32[2048,1536]{1,0:T(8,128)}, f32[2048,1536]{1,0:T(8,128)})) %all-reduce.30.cloned.1.call-update) | async-done | bytes 25165840 | tf_op jit(solution)/shard_map/psum | solution.py:210
  2082.1 26.8 %all_to_all.45 = bf16[8,256,384]{2,1,0:T(8,128)(2,1)} all-to-all(bf16[8,256,384]{2,1,0:T(8,128)(2,1)S(1)} %bitcast.451), channel_id=1, replica_groups=mesh['dp'=8,'tensor'=4] {'dp'}, dimensions={0} | all-to-all | bytes 3145728 | tf_op jit(solution)/shard_map/all_to_all | solution.py:291
  2109.0 24.1 all_to_all.46
  2152.5 38.1 %reduce-scatter.7.cloned.1.call-done = f32[192,2,768]{2,0,1:T(8,128)} async-done(((f32[1536,2,768]{2,0,1:T(8,128)}), f32[192,2,768]{2,0,1:T(8,128)}) %reduce-scatter.7.cloned.1.call-update) | async-done | bytes 1179664 | tf_op jit(solution)/shard_map/reduce_scatter | solution.py:260
  2193.8 25.0 all-reduce.24
  2218.8 88.6 %all-gather.12.cloned.1.call-done = bf16[2048,1536]{1,0:T(8,128)(2,1)} async-done(((bf16[2048,384]{1,0:T(8,128)(2,1)}), bf16[2048,1536]{1,0:T(8,128)(2,1)}) %all-gather.12.cloned.1.call-update) | async-done | bytes 6291472 | tf_op jit(solution)/shard_map/all_gather | solution.py:295
  2307.4 16.8 gather_fusion.3
  2324.2 98.3 %all-gather.10.cloned.1.call-done = bf16[2048,1536]{1,0:T(8,128)(2,1)} async-done(((bf16[2048,384]{1,0:T(8,128)(2,1)}), bf16[2048,1536]{1,0:T(8,128)(2,1)}) %all-gather.10.cloned.1.call-update) | async-done | bytes 6291472 | tf_op jit(solution)/shard_map/all_gather | solution.py:294
  2439.3 23.6 reduce-scatter.9.cloned.1.call-done
  2462.9 57.8 %reduce-scatter.11.cloned.1.call-done = f32[192,768]{1,0:T(8,128)} async-done(((f32[1536,768]{1,0:T(8,128)}), f32[192,768]{1,0:T(8,128)}) %reduce-scatter.11.cloned.1.call-update) | async-done | bytes 589840 | tf_op jit(solution)/shard_map/reduce_scatter | solution.py:263
  (1035 shorter events, 820.6 us)
Async XLA Ops:
  7.2 182.1 %all-gather.6.cloned.1.call-start = ((), (), s32[]{:S(2)}) async-start(), calls=%async_computation.8 | async-start | bytes 5308416 | tf_op jit(solution)/shard_map/all_gather | solution.py:144
  36.4 95.1 %copy-start.73 = (f32[12]{0:T(128)S(1)}, f32[12]{0:T(128)}, u32[]{:S(2)}) copy-start(f32[12]{0:T(128)} %param.34) | copy-start | bytes 148
  36.4 122.0 %all-to-all-start = ((bf16[8,256,1536]{2,1,0:T(8,128)(2,1)}), bf16[8,256,1536]{2,1,0:T(8,128)(2,1)}, u32[]{:S(2)}, u32[]{:S(2)}) async-start(bf16[8,256,1536]{2,1,0:T(8,128)(2,1)} %bitcast.442), calls=%async_computation | async-start | bytes 12582912 | tf_op jit(solution)/shard_map/all_to_all | solution.py:140
  41.6 527.2 %all-gather.8.cloned.1.call-start = ((), (), s32[]{:S(2)}) async-start(), calls=%async_computation.9 | async-start | bytes 2654208 | tf_op jit(solution)/shard_map/all_gather | solution.py:147
  131.6 46.8 %copy-start.15 = (bf16[1536,12]{0,1:T(8,128)(2,1)}, bf16[1536,12]{0,1:T(8,128)(2,1)S(1)}, u32[]{:S(2)}) copy-start(bf16[1536,12]{0,1:T(8,128)(2,1)S(1)} %reshape.579) | copy-start | bytes 110596
  131.6 46.8 %copy-start.60 = (f32[12]{0:T(128)}, f32[12]{0:T(128)S(1)}, u32[]{:S(2)}) copy-start(f32[12]{0:T(128)S(1)} %exp.96) | copy-start | bytes 148
  148.8 62.9 %copy-start.37 = (f32[768]{0:T(1024)}, f32[768]{0:T(1024)S(1)}, u32[]{:S(2)}) copy-start(f32[768]{0:T(1024)S(1)} %get-tuple-element.897) | copy-start | bytes 9220
  148.8 62.8 %copy-start.39 = (f32[768]{0:T(1024)}, f32[768]{0:T(1024)S(1)}, u32[]{:S(2)}) copy-start(f32[768]{0:T(1024)S(1)} %get-tuple-element.898) | copy-start | bytes 9220
  148.8 62.8 %copy-start.41 = (f32[768]{0:T(1024)}, f32[768]{0:T(1024)S(1)}, u32[]{:S(2)}) copy-start(f32[768]{0:T(1024)S(1)} %get-tuple-element.899) | copy-start | bytes 9220
  148.8 62.8 %copy-start.43 = (f32[768]{0:T(1024)}, f32[768]{0:T(1024)S(1)}, u32[]{:S(2)}) copy-start(f32[768]{0:T(1024)S(1)} %get-tuple-element.896) | copy-start | bytes 9220
  158.4 53.3 %copy-start.17 = (f32[2048]{0:T(1024)}, f32[2048]{0:T(1024)S(1)}, u32[]{:S(2)}) copy-start(f32[2048]{0:T(1024)S(1)} %get-tuple-element.1029) | copy-start | bytes 24580
  158.4 53.3 %copy-start.19 = (f32[2048]{0:T(1024)}, f32[2048]{0:T(1024)S(1)}, u32[]{:S(2)}) copy-start(f32[2048]{0:T(1024)S(1)} %get-tuple-element.1030) | copy-start | bytes 24580
  158.4 53.3 %copy-start.21 = (f32[2048]{0:T(1024)}, f32[2048]{0:T(1024)S(1)}, u32[]{:S(2)}) copy-start(f32[2048]{0:T(1024)S(1)} %get-tuple-element.1031) | copy-start | bytes 24580
  158.4 410.3 %all-to-all-start.2 = ((bf16[8,256,1536]{2,1,0:T(8,128)(2,1)}), bf16[8,256,1536]{2,1,0:T(8,128)(2,1)}, u32[]{:S(2)}, u32[]{:S(2)}) async-start(bf16[8,256,1536]{2,1,0:T(8,128)(2,1)} %bitcast.441), calls=%async_computation.2 | async-start | bytes 12582912 | tf_op jit(solution)/shard_map/all_to_all | solution.py:141
  163.2 1905.6 %all-reduce.30.cloned.1.call-start = ((), (), s32[]{:S(2)}) async-start(), calls=%async_computation.16 | async-start | bytes 50331648 | tf_op jit(solution)/shard_map/psum | solution.py:210
  708.9 32.2 %copy-start.36 = (s32[8,256]{1,0:T(8,128)S(1)}, s32[8,256]{1,0:T(8,128)}, u32[]{:S(2)}) copy-start(s32[8,256]{1,0:T(8,128)} %copy-done.35) | copy-start | bytes 24580 | tf_op jit(solution)/shard_map/transpose(jvp())/while
  999.7 32.2 %copy-start.36 = (s32[8,256]{1,0:T(8,128)S(1)}, s32[8,256]{1,0:T(8,128)}, u32[]{:S(2)}) copy-start(s32[8,256]{1,0:T(8,128)} %copy-done.35) | copy-start | bytes 24580 | tf_op jit(solution)/shard_map/transpose(jvp())/while
  1057.9 32.2 %copy-start.36 = (s32[8,256]{1,0:T(8,128)S(1)}, s32[8,256]{1,0:T(8,128)}, u32[]{:S(2)}) copy-start(s32[8,256]{1,0:T(8,128)} %copy-done.35) | copy-start | bytes 24580 | tf_op jit(solution)/shard_map/transpose(jvp())/while
  1126.3 33.3 %slice-start = ((s8[6291456]{0:T(1024)(128)(4,1)}), s8[4194304]{0:T(1024)(128)(4,1)S(1)}, s32[]{:S(2)}) async-start(s8[6291456]{0:T(1024)(128)(4,1)} %bitcast.432), calls=%async_computation.17 | async-start | bytes 8388608
  1167.9 983.0 %reduce-scatter.13.cloned.1.call-start = ((), (), s32[]{:S(2)}) async-start(), calls=%async_computation.15 | async-start | bytes 884736
  1189.7 1000.9 %reduce-scatter.7.cloned.1.call-start = ((), (), s32[]{:S(2)}) async-start(), calls=%async_computation.12 | async-start | bytes 10616832 | tf_op jit(solution)/shard_map/reduce_scatter | solution.py:260
  1205.4 1102.0 %all-gather.12.cloned.1.call-start = ((), (), s32[]{:S(2)}) async-start(), calls=%async_computation.11 | async-start | bytes 7864320 | tf_op jit(solution)/shard_map/all_gather | solution.py:295
  1218.5 850.4 %copy-start.11 = (bf16[1536,256]{1,0:T(8,128)(2,1)S(1)}, bf16[1536,256]{1,0:T(8,128)(2,1)}, u32[]{:S(2)}) copy-start(bf16[1536,256]{1,0:T(8,128)(2,1)} %copy-done.10) | copy-start | bytes 2359300
  1218.5 850.4 %copy-start.29 = (f32[2048]{0:T(1024)S(1)}, f32[2048]{0:T(1024)}, u32[]{:S(2)}) copy-start(f32[2048]{0:T(1024)} %copy-done.28) | copy-start | bytes 24580
  1218.5 850.4 %copy-start.31 = (f32[1536]{0:T(1024)S(1)}, f32[1536]{0:T(1024)}, u32[]{:S(2)}) copy-start(f32[1536]{0:T(1024)} %param.25) | copy-start | bytes 18436
  2082.0 51.1 %copy-start.12 = (bf16[2048,256]{1,0:T(8,128)(2,1)S(1)}, bf16[2048,256]{1,0:T(8,128)(2,1)}, u32[]{:S(2)}) copy-start(bf16[2048,256]{1,0:T(8,128)(2,1)} %get-tuple-element.971) | copy-start | bytes 3145732
  2108.9 313.6 %all-gather.10.cloned.1.call-start = ((), (), s32[]{:S(2)}) async-start(), calls=%async_computation.10 | async-start | bytes 7864320 | tf_op jit(solution)/shard_map/all_gather | solution.py:294
  2133.1 329.8 %reduce-scatter.9.cloned.1.call-start = ((), (), s32[]{:S(2)}) async-start(), calls=%async_computation.13 | async-start | bytes 1769472 | tf_op jit(solution)/shard_map/reduce_scatter | solution.py:261
  2139.0 381.7 %reduce-scatter.11.cloned.1.call-start = ((), (), s32[]{:S(2)}) async-start(), calls=%async_computation.14 | async-start | bytes 5308416 | tf_op jit(solution)/shard_map/reduce_scatter | solution.py:263
  2150.7 43.0 %copy-start.49 = (f32[12]{0:T(128)S(1)}, f32[12]{0:T(128)}, u32[]{:S(2)}) copy-start(f32[12]{0:T(128)} %get-tuple-element.530) | copy-start | bytes 148
  2150.7 43.0 %copy-start.65 = (f32[768]{0:T(1024)S(1)}, f32[768]{0:T(1024)}, u32[]{:S(2)}) copy-start(f32[768]{0:T(1024)} %get-tuple-element.882) | copy-start | bytes 9220
  2150.7 156.6 %copy-start.34 = (s32[2048]{0:T(1024)S(1)}, s32[2048]{0:T(1024)}, u32[]{:S(2)}) copy-start(s32[2048]{0:T(1024)} %get-tuple-element.987) | copy-start | bytes 24580
  (105 other events, 1154.9 us)
Sparse Core Ops, SparseCore 0:
  10.4 46.6 all-gather.5
  59.0 70.6 all-gather.7
  1168.0 900.7 all-reduce.29
  2072.4 38.3 reduce-scatter.12
  2114.2 76.3 reduce-scatter.6
  2192.0 115.3 all-gather.11
  2308.9 113.5 all-gather.9
  2426.3 36.5 reduce-scatter.8
  2466.9 53.7 reduce-scatter.10
where the time goes:
time: 2550 us; the launch traced here: 2530 us
  waiting for transfers between devices  1010 us (40%)
  local copies, waits for them, and re-layouts  624 us (24%)
  blocking collectives  342 us (13%)
  matrix products  315 us (12%)
  other arithmetic  188 us (7%)
    psum x1, waiting for transfers between devices, on_device(): branch = lax.psum(partial_out, 'tensor')  702 us
    dynamic_update_slice x72, local copies, waits for them, and re-layouts, mixer(): lax.scan(jax.checkpoint(span_step), initial, (blocked(values), blocked(wr...  344 us
    psum x1, blocking collectives, on_device(): lax.psum((shared_part, shared_filter_part, shared_bias_part), 'tensor')  147 us
    dot_general x24, matrix products, span_step(): local_out = jnp.einsum('hts,shp->thp', mixing, value_blk, precision=PRECISE)  101 us
    all_gather x1, waiting for transfers between devices, on_device(): lax.all_gather(part_out, 'tensor', axis=1, tiled=True)  98.3 us
    all_gather x1, blocking collectives, on_device(): lax.all_gather(step_weight.astype(jnp.bfloat16), 'dp', axis=0, tiled=True)  88.8 us
    all_gather x1, waiting for transfers between devices, on_device(): lax.all_gather(part_grad, 'tensor', axis=1, tiled=True)  88.6 us
    reduce_scatter x1, waiting for transfers between devices, on_device(): lax.psum_scatter(out_grad, 'dp', scatter_dimension=0, tiled=True)  57.8 us
  transfers between devices with their start and end apart: 11, of which 6 were waited for; matrix products, arithmetic and copies ran while one was open for 21% of the time, Pallas kernels for 0%

commit v1 on v0

--- a/solution.py
+++ b/solution.py
@@ -207,7 +207,20 @@
     gate_scale = lax.rsqrt(square_sum / INNER + EPSILON)[:, None]
     gate_normed = (gated * gate_scale * gate_gain).astype(jnp.bfloat16)
     partial_out = jnp.einsum("ti,di->td", gate_normed, out_full, preferred_element_type=jnp.float32)
-    branch = lax.psum(partial_out, "tensor")
+
+    def _launch_heaps(view, named_axis):
+        k_all = jax.lax.axis_size(named_axis)
+
+        def _shape_sizes(reached, moved):
+            if moved >= k_all:
+                return reached
+            back = tuple(((at, at ^ moved) for at in range(k_all)))
+            now = jax.lax.ppermute(reached, named_axis, back)
+            return _shape_sizes(reached + now, 2 * moved)
+
+        return _shape_sizes(view, 1)
+
+    branch = _launch_heaps(partial_out, "tensor")
     layer_work = (hidden_in + branch).astype(jnp.bfloat16)
     part_out = lax.dynamic_slice_in_dim(layer_work, column, col_share, 1)
     out_grad = jnp.einsum("td,ti->di", work_cot, gate_normed, preferred_element_type=jnp.float32)

time: 2550 us -> 2820 us (1.11)
  blocking collectives: 342 us -> 804 us
  waiting for transfers between devices: 1010 us -> 815 us
    psum x1, waiting for transfers between devices: 702 us -> 0.01 us  [on_device(): normed_back = lax.psum(input_part, 'tensor')]
    ppermute x0 -> x2, waiting for transfers between devices: none -> 593 us  [_shape_sizes(): now = jax.lax.ppermute(reached, named_axis, back)]
    psum x1, blocking collectives: 147 us -> 611 us  [on_device(): lax.psum((shared_part, shared_filter_part, shared_bias_part), 'tensor')]
    all_gather x1, waiting for transfers between devices: 88.6 us -> 42.4 us  [on_device(): lax.all_gather(part_grad, 'tensor', axis=1, tiled=True)]
    reduce_scatter x1, waiting for transfers between devices: 38.1 us -> 0.01 us  [on_device(): lax.psum_scatter(inner_grad, 'dp', scatter_dimension=0, tiled=True)]
  transfers between devices with their start and end apart: 11 -> 13, of which waited for: 6 -> 5; matrix products, arithmetic and copies ran while one was open for 21% -> 20% of each run, Pallas kernels for 0% -> 0%
where the time goes in v1:
time: 2820 us; the launch traced here: 2800 us
  waiting for transfers between devices  815 us (29%)
  blocking collectives  804 us (29%)
  local copies, waits for them, and re-layouts  624 us (22%)
  matrix products  310 us (11%)
  other arithmetic  198 us (7%)
    psum x1, blocking collectives, on_device(): lax.psum((shared_part, shared_filter_part, shared_bias_part), 'tensor')  611 us
    ppermute x2, waiting for transfers between devices, _shape_sizes(): now = jax.lax.ppermute(reached, named_axis, back)  593 us
    dynamic_update_slice x72, local copies, waits for them, and re-layouts, mixer(): lax.scan(jax.checkpoint(span_step), initial, (blocked(values), blocked(wr...  345 us
    dot_general x24, matrix products, span_step(): local_out = jnp.einsum('hts,shp->thp', mixing, value_blk, precision=PRECISE)  101 us
    all_gather x1, waiting for transfers between devices, on_device(): lax.all_gather(part_out, 'tensor', axis=1, tiled=True)  98.3 us
    all_gather x1, blocking collectives, on_device(): lax.all_gather(step_weight.astype(jnp.bfloat16), 'dp', axis=0, tiled=True)  88.7 us
    reduce_scatter x1, waiting for transfers between devices, on_device(): lax.psum_scatter(out_grad, 'dp', scatter_dimension=0, tiled=True)  57.8 us
  transfers between devices with their start and end apart: 13, of which 5 were waited for; matrix products, arithmetic and copies ran while one was open for 20% of the time, Pallas kernels for 0%

profile of v1, /device:TPU:0, one launch (start us, length us, event | category | flops | bytes accessed | tf_op | source)
XLA Modules:
  0.0 2803.3 jit_solution(15248362805198247531)
XLA Ops:
  19.1 17.3 gather_fusion
  42.7 88.7 %all-gather = bf16[8,192,12]{1,2,0:T(8,128)(2,1)S(1)} all-gather(bf16[1,192,12]{1,2,0:T(8,128)(2,1)S(1)} %convert_bitcast_fusion), channel_id=1, replica_groups=mesh['dp'=8,'tensor'=4] {'dp'}, dimensions={0}, use_global_device_ids=true | all-gather | bytes 41472 | tf_op jit(solution)/shard_map/all_gather | solution.py:146
  131.8 16.9 gather_fusion.2
  240.3 295.2 %while.47 = (s32[]{:T(128)}, f32[12,128,64]{1,2,0:T(8,128)S(1)}, s32[]{:T(128)}, f32[8,256,12,64]{1,0,3,2:T(8,128)}, f32[8,12,128,64]{2,3,1,0:T(8,128)}, /*index...) while((s32[]{:T(128)}, f32[12,128,64]{1,2,0:T(8,128)S(1)}, ...), condition=%wide.region_8.9_spmd.clone, body=%wide.region_5.8_spmd.clone.sunk | while | flops 1313649664 | bytes 11765497 | solution.py:87
  254.1 18.5 dynamic_update_slice.85
  291.0 18.5 dynamic_update_slice.85
  327.9 18.5 dynamic_update_slice.85
  364.8 18.5 dynamic_update_slice.85
  401.7 18.5 dynamic_update_slice.85
  438.6 18.5 dynamic_update_slice.85
  475.5 18.5 dynamic_update_slice.85
  512.4 18.5 dynamic_update_slice.85
  625.6 466.3 %while.48 = (s32[]{:T(128)}, f32[12]{0:T(128)}, f32[12,128,64]{1,2,0:T(8,128)S(1)}, f32[8,256,12,64]{1,0,3,2:T(8,128)}, f32[8,256,128]{2,1,0:T(8,128)}, /*index=...) while((s32[]{:T(128)}, f32[12]{0:T(128)}, ...), condition=%wide.region_26.27_spmd.clone, body=%wide.region_13.26_spmd.clone.sunk | while | flops 3037355008 | bytes 28656244 | solution.py:87
  658.2 18.5 dynamic_update_slice.89
  716.5 18.5 dynamic_update_slice.89
  774.7 18.5 dynamic_update_slice.89
  832.9 18.5 dynamic_update_slice.89
  891.1 18.5 dynamic_update_slice.89
  949.3 18.5 dynamic_update_slice.89
  1007.5 18.5 dynamic_update_slice.89
  1065.7 18.5 dynamic_update_slice.89
  1107.1 16.9 multiply_reduce_fusion.13
  1181.7 593.2 %collective-permute-done = f32[2048,1536]{1,0:T(8,128)} collective-permute-done((f32[2048,1536]{1,0:T(8,128)}, f32[2048,1536]{1,0:T(8,128)}, u32[]{:S(2)}, u32[]{:S(2)}) %collective-permute-start) | collective-permute-done | bytes 12582944 | tf_op jit(solution)/shard_map/ppermute | solution.py:218
  1819.3 610.9 %all-reduce.30 = (bf16[2048,256]{1,0:T(8,128)(2,1)}, f32[4,256]{1,0:T(4,128)S(1)}, f32[256]{0:T(256)S(1)}) all-reduce(f32[2048,256]{1,0:T(8,128)S(1)} %fusion.112, f32[4,256]{1,0:T(4,128)S(1)} %pad_add_fusion.1, f32[256]{0:T(256)S(1)} %get-tuple-element.895), channel_id=1, replica_groups=mesh['dp'=8,'tensor'=4] {'tensor'}, use_global_device_ids=true, to_apply=%region_28.29 | all-reduce | flops 525568 | bytes 3155968 | tf_op jit(solution)/shard_map/psum | solution.py:246
  2444.2 25.3 all_to_all.45
  2469.5 24.1 all_to_all.46
  2512.4 25.1 all-reduce.24
  2540.7 42.4 %all-gather.12.cloned.1.call-done = bf16[2048,1536]{1,0:T(8,128)(2,1)} async-done(((bf16[2048,384]{1,0:T(8,128)(2,1)}), bf16[2048,1536]{1,0:T(8,128)(2,1)}) %all-gather.12.cloned.1.call-update) | async-done | bytes 6291472 | tf_op jit(solution)/shard_map/all_gather | solution.py:308
  2583.1 16.8 gather_fusion.3
  2599.9 98.3 %all-gather.10.cloned.1.call-done = bf16[2048,1536]{1,0:T(8,128)(2,1)} async-done(((bf16[2048,384]{1,0:T(8,128)(2,1)}), bf16[2048,1536]{1,0:T(8,128)(2,1)}) %all-gather.10.cloned.1.call-update) | async-done | bytes 6291472 | tf_op jit(solution)/shard_map/all_gather | solution.py:307
  2715.1 23.6 reduce-scatter.9.cloned.1.call-done
  2738.6 57.8 %reduce-scatter.11.cloned.1.call-done = f32[192,768]{1,0:T(8,128)} async-done(((f32[1536,768]{1,0:T(8,128)}), f32[192,768]{1,0:T(8,128)}) %reduce-scatter.11.cloned.1.call-update) | async-done | bytes 589840 | tf_op jit(solution)/shard_map/reduce_scatter | solution.py:276
  (1035 shorter events, 810.7 us)
Async XLA Ops:
  7.2 182.2 %all-gather.6.cloned.1.call-start = ((), (), s32[]{:S(2)}) async-start(), calls=%async_computation.8 | async-start | bytes 5308416 | tf_op jit(solution)/shard_map/all_gather | solution.py:144
  36.4 95.1 %copy-start.73 = (f32[12]{0:T(128)S(1)}, f32[12]{0:T(128)}, u32[]{:S(2)}) copy-start(f32[12]{0:T(128)} %param.34) | copy-start | bytes 148
  36.5 122.0 %all-to-all-start = ((bf16[8,256,1536]{2,1,0:T(8,128)(2,1)}), bf16[8,256,1536]{2,1,0:T(8,128)(2,1)}, u32[]{:S(2)}, u32[]{:S(2)}) async-start(bf16[8,256,1536]{2,1,0:T(8,128)(2,1)} %bitcast.440), calls=%async_computation | async-start | bytes 12582912 | tf_op jit(solution)/shard_map/all_to_all | solution.py:140
  41.6 528.3 %all-gather.8.cloned.1.call-start = ((), (), s32[]{:S(2)}) async-start(), calls=%async_computation.9 | async-start | bytes 2654208 | tf_op jit(solution)/shard_map/all_gather | solution.py:147
  131.6 46.9 %copy-start.16 = (bf16[1536,12]{0,1:T(8,128)(2,1)}, bf16[1536,12]{0,1:T(8,128)(2,1)S(1)}, u32[]{:S(2)}) copy-start(bf16[1536,12]{0,1:T(8,128)(2,1)S(1)} %reshape.579) | copy-start | bytes 110596
  131.6 46.9 %copy-start.61 = (f32[12]{0:T(128)}, f32[12]{0:T(128)S(1)}, u32[]{:S(2)}) copy-start(f32[12]{0:T(128)S(1)} %exp.96) | copy-start | bytes 148
  148.8 62.9 %copy-start.38 = (f32[768]{0:T(1024)}, f32[768]{0:T(1024)S(1)}, u32[]{:S(2)}) copy-start(f32[768]{0:T(1024)S(1)} %get-tuple-element.897) | copy-start | bytes 9220
  148.8 62.9 %copy-start.40 = (f32[768]{0:T(1024)}, f32[768]{0:T(1024)S(1)}, u32[]{:S(2)}) copy-start(f32[768]{0:T(1024)S(1)} %get-tuple-element.898) | copy-start | bytes 9220
  148.9 62.9 %copy-start.42 = (f32[768]{0:T(1024)}, f32[768]{0:T(1024)S(1)}, u32[]{:S(2)}) copy-start(f32[768]{0:T(1024)S(1)} %get-tuple-element.899) | copy-start | bytes 9220
  148.9 62.9 %copy-start.44 = (f32[768]{0:T(1024)}, f32[768]{0:T(1024)S(1)}, u32[]{:S(2)}) copy-start(f32[768]{0:T(1024)S(1)} %get-tuple-element.896) | copy-start | bytes 9220
  158.4 53.3 %copy-start.18 = (f32[2048]{0:T(1024)}, f32[2048]{0:T(1024)S(1)}, u32[]{:S(2)}) copy-start(f32[2048]{0:T(1024)S(1)} %get-tuple-element.1027) | copy-start | bytes 24580
  158.5 53.3 %copy-start.20 = (f32[2048]{0:T(1024)}, f32[2048]{0:T(1024)S(1)}, u32[]{:S(2)}) copy-start(f32[2048]{0:T(1024)S(1)} %get-tuple-element.1028) | copy-start | bytes 24580
  158.5 53.3 %copy-start.22 = (f32[2048]{0:T(1024)}, f32[2048]{0:T(1024)S(1)}, u32[]{:S(2)}) copy-start(f32[2048]{0:T(1024)S(1)} %get-tuple-element.1029) | copy-start | bytes 24580
  158.5 411.4 %all-to-all-start.2 = ((bf16[8,256,1536]{2,1,0:T(8,128)(2,1)}), bf16[8,256,1536]{2,1,0:T(8,128)(2,1)}, u32[]{:S(2)}, u32[]{:S(2)}) async-start(bf16[8,256,1536]{2,1,0:T(8,128)(2,1)} %bitcast.439), calls=%async_computation.2 | async-start | bytes 12582912 | tf_op jit(solution)/shard_map/all_to_all | solution.py:141
  163.3 2266.9 %all-reduce.29.cloned.1.call-start = ((), (), s32[]{:S(2)}) async-start(), calls=%async_computation.11 | async-start | bytes 25165824 | tf_op jit(solution)/shard_map/psum | solution.py:256
  710.1 32.1 %copy-start.37 = (s32[8,256]{1,0:T(8,128)S(1)}, s32[8,256]{1,0:T(8,128)}, u32[]{:S(2)}) copy-start(s32[8,256]{1,0:T(8,128)} %copy-done.36) | copy-start | bytes 24580 | tf_op jit(solution)/shard_map/transpose(jvp())/while
  768.4 32.1 %copy-start.37 = (s32[8,256]{1,0:T(8,128)S(1)}, s32[8,256]{1,0:T(8,128)}, u32[]{:S(2)}) copy-start(s32[8,256]{1,0:T(8,128)} %copy-done.36) | copy-start | bytes 24580 | tf_op jit(solution)/shard_map/transpose(jvp())/while
  826.6 32.1 %copy-start.37 = (s32[8,256]{1,0:T(8,128)S(1)}, s32[8,256]{1,0:T(8,128)}, u32[]{:S(2)}) copy-start(s32[8,256]{1,0:T(8,128)} %copy-done.36) | copy-start | bytes 24580 | tf_op jit(solution)/shard_map/transpose(jvp())/while
  1059.4 32.1 %copy-start.37 = (s32[8,256]{1,0:T(8,128)S(1)}, s32[8,256]{1,0:T(8,128)}, u32[]{:S(2)}) copy-start(s32[8,256]{1,0:T(8,128)} %copy-done.36) | copy-start | bytes 24580 | tf_op jit(solution)/shard_map/transpose(jvp())/while
  1149.8 1361.0 %reduce-scatter.13.cloned.1.call-start = ((), (), s32[]{:S(2)}) async-start(), calls=%async_computation.16 | async-start | bytes 884736
  1162.3 612.7 %collective-permute-start = (f32[2048,1536]{1,0:T(8,128)}, f32[2048,1536]{1,0:T(8,128)}, u32[]{:S(2)}, u32[]{:S(2)}) collective-permute-start(f32[2048,1536]{1,0:T(8,128)} %fusion.136), channel_id=1, source_target_pairs={{0,1},{1,0},{2,3},{3,2},{4,5},{5,4},{6,7},{7,6},{8,9},{9,8},{10,11... | collective-permute-start | bytes 37748744 | tf_op jit(solution)/shard_map/ppermute | solution.py:218
  1181.7 1355.8 %reduce-scatter.7.cloned.1.call-start = ((), (), s32[]{:S(2)}) async-start(), calls=%async_computation.13 | async-start | bytes 10616832 | tf_op jit(solution)/shard_map/reduce_scatter | solution.py:273
  1789.7 649.6 %collective-permute-start.1 = (f32[2048,1536]{1,0:T(8,128)}, f32[2048,1536]{1,0:T(8,128)}, u32[]{:S(2)}, u32[]{:S(2)}) collective-permute-start(f32[2048,1536]{1,0:T(8,128)} %add.264), channel_id=1, source_target_pairs={{0,2},{1,3},{2,0},{3,1},{4,6},{5,7},{6,4},{7,5},{8,10},{9,11},{10,... | collective-permute-start | bytes 37748744 | tf_op jit(solution)/shard_map/ppermute | solution.py:218
  1805.4 777.7 %all-gather.12.cloned.1.call-start = ((), (), s32[]{:S(2)}) async-start(), calls=%async_computation.12 | async-start | bytes 7864320 | tf_op jit(solution)/shard_map/all_gather | solution.py:308
  1818.6 611.7 %copy-start.12 = (bf16[1536,256]{1,0:T(8,128)(2,1)S(1)}, bf16[1536,256]{1,0:T(8,128)(2,1)}, u32[]{:S(2)}) copy-start(bf16[1536,256]{1,0:T(8,128)(2,1)} %copy-done.11) | copy-start | bytes 2359300
  1818.6 611.6 %copy-start.30 = (f32[2048]{0:T(1024)S(1)}, f32[2048]{0:T(1024)}, u32[]{:S(2)}) copy-start(f32[2048]{0:T(1024)} %copy-done.29) | copy-start | bytes 24580
  1818.6 611.6 %copy-start.32 = (f32[1536]{0:T(1024)S(1)}, f32[1536]{0:T(1024)}, u32[]{:S(2)}) copy-start(f32[1536]{0:T(1024)} %param.25) | copy-start | bytes 18436
  2444.2 49.5 %copy-start.13 = (bf16[2048,256]{1,0:T(8,128)(2,1)S(1)}, bf16[2048,256]{1,0:T(8,128)(2,1)}, u32[]{:S(2)}) copy-start(bf16[2048,256]{1,0:T(8,128)(2,1)} %get-tuple-element.971) | copy-start | bytes 3145732
  2469.5 228.7 %all-gather.10.cloned.1.call-start = ((), (), s32[]{:S(2)}) async-start(), calls=%async_computation.10 | async-start | bytes 7864320 | tf_op jit(solution)/shard_map/all_gather | solution.py:307
  2493.7 245.0 %reduce-scatter.9.cloned.1.call-start = ((), (), s32[]{:S(2)}) async-start(), calls=%async_computation.14 | async-start | bytes 1769472 | tf_op jit(solution)/shard_map/reduce_scatter | solution.py:274
  2499.7 296.8 %reduce-scatter.11.cloned.1.call-start = ((), (), s32[]{:S(2)}) async-start(), calls=%async_computation.15 | async-start | bytes 5308416 | tf_op jit(solution)/shard_map/reduce_scatter | solution.py:276
  2510.6 72.5 %copy-start.35 = (s32[2048]{0:T(1024)S(1)}, s32[2048]{0:T(1024)}, u32[]{:S(2)}) copy-start(s32[2048]{0:T(1024)} %get-tuple-element.985) | copy-start | bytes 24580
  (105 other events, 1102.1 us)
Sparse Core Ops, SparseCore 0:
  10.4 46.6 all-gather.5
  59.6 70.0 all-gather.7
  1149.9 719.2 all-reduce.28
  1872.8 38.8 reduce-scatter.12
  1915.0 76.6 reduce-scatter.6
  2469.6 113.4 all-gather.11
  2584.7 113.4 all-gather.9
  2702.1 36.5 reduce-scatter.8
  2742.7 53.7 reduce-scatter.10
